TPU v7x, 32 devices: a whole 2x2x4 slice. The times are simulated.
32 devices in a mesh: chan: 16 (over z, y, core), band: 2 (over x).
Axes of the slice: x: 2, y: 2, z: 4, core: 2. Of those that a mesh axis runs over, the one named last changes fastest.
Arguments:
- strain: bfloat16 [4096, 4, 4096], P('chan', None, 'band'), may hold values from -6 to 6
- band_start: int32 [2], replicated, may hold values from 4 to 818
Outputs:
- coherency: bfloat16 [2, 2, 4096, 4096], P('band', None, 'chan')
All inputs are finite; a program needn't handle non-finite values.
Results may differ from a plain program's by a relative error of at most 0.0056.
Values may be sent and summed in bfloat16 or wider, within the bound.
A program may use at most 64 MiB of HBM per device.

v0:
```python
import math
import jax
import jax.numpy as jnp
from jax import lax
from jax.sharding import PartitionSpec as P

WINDOW_SAMPLES = 4096
K = 32


def dft_table(freqs, positions):
    phase_angles = positions[:, None, None] * freqs[None, :, :] % WINDOW_SAMPLES
    angles = phase_angles.astype(jnp.float32) * (2.0 * math.pi / WINDOW_SAMPLES)
    taper = 0.5 - 0.5 * jnp.cos(positions.astype(jnp.float32) * (2.0 * math.pi / WINDOW_SAMPLES))
    cosine = taper[:, None, None] * jnp.cos(angles)
    sine = -taper[:, None, None] * jnp.sin(angles)
    return jnp.concatenate([cosine, sine], axis=2).astype(jnp.bfloat16)


def whiten(spectrum, chans, windows):
    power = jnp.mean(spectrum * spectrum, axis=1, keepdims=True)
    whitened = (spectrum * lax.rsqrt(power + 1e-06)).astype(jnp.bfloat16)
    return (
        whitened.reshape(chans, windows, 2, K).transpose(0, 2, 1, 3).reshape(chans, 2 * windows * K)
    )


def cross_block(local_panel_rows, other_panel):
    half_feat = other_panel.shape[1] // 2
    rotated = jnp.concatenate([-other_panel[:, half_feat:], other_panel[:, :half_feat]], axis=1)
    stacked_spectra = jnp.stack([other_panel, rotated])
    cross_product = jnp.einsum(
        "gb,ozb->ogz", local_panel_rows, stacked_spectra, preferred_element_type=jnp.float32
    )
    return (cross_product * (1.0 / (2.0 * K))).astype(jnp.bfloat16)


def shards(strain, band_start):
    chans, windows, samp_dev = strain.shape
    flat = strain.reshape(chans * windows, samp_dev)
    band_index = lax.axis_index("band")
    bins = jnp.arange(K, dtype=jnp.int32)
    positions = band_index * samp_dev + jnp.arange(samp_dev, dtype=jnp.int32)
    own_rows = band_start.shape[0] // lax.axis_size("band")
    table = dft_table(band_start[:, None] + bins[None, :], positions)
    partial_sum = jnp.dot(
        flat,
        table.reshape(samp_dev, own_rows * lax.axis_size("band") * 2 * K),
        preferred_element_type=jnp.float32,
    )
    spectrum = lax.psum_scatter(
        partial_sum.reshape(chans * windows, own_rows * lax.axis_size("band"), 2 * K).transpose(
            1, 0, 2
        ),
        "band",
        scatter_dimension=0,
        tiled=True,
    )[0]
    panel = whiten(spectrum, chans, windows)
    result = cross_block(panel, lax.all_gather(panel, "chan", axis=0, tiled=True))
    return result[None]


def solution(mesh):
    return jax.shard_map(
        shards,
        mesh=mesh,
        in_specs=(P("chan", None, "band"), P()),
        out_specs=P("band", None, "chan", None),
        check_vma=False,
    )
```

profile of v0, /device:TPU:0, one launch (start us, length us, event | category | flops | bytes accessed | tf_op | source)
XLA Modules:
  0.0 110.6 jit_solution(17581041792112892675)
XLA Ops:
  6.5 0.0 reduce-scatter.2.cloned.1.call-start
  6.5 0.1 multiply_subtract_fusion
  6.6 0.7 iota_add_fusion.1
  7.3 6.9 %reshape.73 = bf16[1024,2048]{1,0:T(8,128)(2,1)} reshape(bf16[256,4,2048]{2,1,0:T(4,128)(2,1)} %param.2) | data formatting | bytes 8388608 | tf_op jit(solution)/shard_map/reshape | solution.py:40
  14.2 2.3 %multiply_convert_fusion.3 = (bf16[2048,2,32]{0,2,1:T(8,128)(2,1)S(1)}, bf16[2048,2,32]{0,2,1:T(8,128)(2,1)S(1)}) fusion(s32[2,32]{1,0:T(2,128)S(1)} %iota_add_fusion.1, s32[2048]{0:T(1024)S(1)} %iota_add_fusion, f32[2048]{0:T(1024)S(1)} %get-tuple-element.9, f32[2048]{0:T(1024)S(1)} %get-tuple-element.10), kind=kLoop, calls=%fused_computation.20 | loop fusion | flops 2359296 | bytes 549120 | tf_op jit(solution)/shard_map/convert
  16.5 3.7 %fusion.10 = f32[128,1024]{1,0:T(8,128)S(1)} fusion(bf16[2048,128]{0,1:T(8,128)(2,1)S(1)} %bitcast.22, bf16[1024,2048]{1,0:T(8,128)(2,1)} %reshape.73), kind=kOutput, calls=%fused_computation.27 | convolution fusion | flops 536870912 | bytes 5242880 | tf_op jit(solution)/shard_map/dot_general | solution.py:46
  20.2 1.3 %copy.5 = f32[1024,2,64]{2,0,1:T(8,128)} copy(f32[1024,2,64]{0,2,1:T(8,128)S(1)} %bitcast.21) | data formatting | bytes 1048576 | tf_op jit(solution)/shard_map/reshape | solution.py:52
  21.5 0.0 reduce-scatter.2.cloned.1.call-update
  21.6 0.0 all-gather.2.cloned.1.call-start
  21.6 23.2 %reduce-scatter.2.cloned.1.call-done = f32[1,1024,64]{2,1,0:T(8,128)} async-done(((f32[2,1024,64]{2,1,0:T(8,128)}), f32[1,1024,64]{2,1,0:T(8,128)}) %reduce-scatter.2.cloned.1.call-update) | async-done | bytes 262160 | tf_op jit(solution)/shard_map/reduce_scatter | solution.py:51
  44.8 1.2 %multiply_reduce_fusion = f32[1024]{0:T(1024)S(1)} fusion(f32[1,1024,64]{2,1,0:T(8,128)} %reduce-scatter.2.cloned.1.call-done), kind=kLoop, calls=%fused_computation.18 | loop fusion | flops 130048 | bytes 266240 | tf_op jit(solution)/shard_map/reduce_sum | solution.py:21
  46.1 0.1 rsqrt.12
  46.2 1.7 %squeeze.3 = f32[256,4,2,32]{3,2,1,0:T(2,128)S(1)} reshape(f32[1,1024,64]{2,1,0:T(8,128)} %reduce-scatter.2.cloned.1.call-done) | data formatting | bytes 524288 | tf_op jit(solution)/shard_map/squeeze | solution.py:51
  47.9 1.7 %fusion.7 = bf16[256,2,4,32]{3,1,2,0:T(2,128)(2,1)S(1)} fusion(f32[256,4,2,32]{3,2,1,0:T(2,128)S(1)} %squeeze.3, f32[256,4]{1,0:T(8,128)S(1)} %rsqrt.12), kind=kLoop, calls=%fused_computation.16 | loop fusion | flops 131072 | bytes 397312 | tf_op jit(solution)/shard_map/transpose | solution.py:24
  49.6 0.5 copy.6
  50.1 0.8 copy.7
  50.8 0.0 all-gather.2.cloned.1.call-update
  50.9 41.6 %all-gather.2.cloned.1.call-done = bf16[4096,256]{1,0:T(8,128)(2,1)} async-done(((bf16[256,256]{1,0:T(8,128)(2,1)}), bf16[4096,256]{1,0:T(8,128)(2,1)}) %all-gather.2.cloned.1.call-update) | async-done | bytes 2097168 | tf_op jit(solution)/shard_map/all_gather | solution.py:60
  92.5 0.0 copy-start
  92.5 1.9 %slice_negate_fusion = (bf16[4096,128]{1,0:T(8,128)(2,1)S(1)}, bf16[4096,128]{1,0:T(8,128)(2,1)S(1)}) fusion(bf16[4096,256]{1,0:T(8,128)(2,1)} %all-gather.2.cloned.1.call-done), kind=kLoop, calls=%fused_computation.6 | loop fusion | flops 524288 | bytes 4194304 | tf_op jit(solution)/shard_map/neg | solution.py:30
  94.4 0.2 maximum_bitcast_fusion
  94.6 0.1 copy-done
  94.7 2.7 %fusion = bf16[1,2,256,4096]{2,3,1,0:T(8,128)(2,1)} fusion(bf16[256,256,1]{0,1,2:T(8,128)(2,1)S(1)} %bitcast.25, bf16[1,4096,256]{2,1,0:T(8,128)(2,1)S(1)} %maximum_bitcast_fusion, bf16[1,4096,256]{2,1,0:T(8,128)(2,1)S(1)} %bitcast.23), kind=kOutput, calls=%fused_computation.1 | convolution fusion | flops 1080033280 | bytes 8519680 | tf_op jit(solution)/shard_map/gb,ozb->ogz/dot_general | solution.py:32
  97.4 6.3 %copy.9 = bf16[1,2,256,4096]{3,2,1,0:T(8,128)(2,1)} copy(bf16[1,2,256,4096]{2,3,1,0:T(8,128)(2,1)} %fusion) | data formatting | bytes 8388608 | tf_op jit(solution)/shard_map/broadcast_in_dim | solution.py:61
  (3 shorter events, 0.0 us)
Async XLA Ops:
  6.5 38.3 %reduce-scatter.2.cloned.1.call-start = ((), (), s32[]{:S(2)}) async-start(), calls=%async_computation.1 | async-start | bytes 1572864 | tf_op jit(solution)/shard_map/reduce_scatter | solution.py:51
  21.6 70.9 %all-gather.2.cloned.1.call-start = ((), (), s32[]{:S(2)}) async-start(), calls=%async_computation.2 | async-start | bytes 2228224 | tf_op jit(solution)/shard_map/all_gather | solution.py:60
  92.5 2.2 %copy-start = (bf16[4096,256]{1,0:T(8,128)(2,1)S(1)}, bf16[4096,256]{1,0:T(8,128)(2,1)}, u32[]{:S(2)}) copy-start(bf16[4096,256]{1,0:T(8,128)(2,1)} %all-gather.2.cloned.1.call-done) | copy-start | bytes 6291460
Sparse Core Ops, SparseCore 0:
  21.7 23.0 reduce-scatter.1
  51.0 41.4 all-gather.1
where the time goes:
time: 111 us
  waiting for transfers between devices  64.9 us (58%)
  local copies, waits for them, and re-layouts  17.6 us (16%)
  between operations  13.5 us (12%)
  other arithmetic  8.16 us (7%)
  matrix products  6.46 us (6%)
    all_gather x1, waiting for transfers between devices, shards(): lax.all_gather(panel, 'chan', axis=0, tiled=True)  41.6 us
    reduce_scatter x1, waiting for transfers between devices, shards(): lax.psum_scatter(partial_sum.reshape(chans * windows, own_rows * lax.axis...  23.2 us
    reshape x1, local copies, waits for them, and re-layouts, shards(): flat = strain.reshape(chans * windows, samp_dev)  6.86 us
    broadcast_in_dim x1, local copies, waits for them, and re-layouts, shards(): return result[None]  6.31 us
    dot_general x1, matrix products, shards(): jnp.dot(flat, table.reshape(samp_dev, own_rows * lax.axis_size('band') *...  3.73 us
    dot_general x1, matrix products, cross_block(): jnp.einsum('gb,ozb->ogz', local_panel_rows, stacked_spectra, preferred_el...  2.73 us
    another operation x1, other arithmetic  2.25 us
  transfers between devices with their start and end apart: 2, of which 2 were waited for; matrix products, arithmetic and copies ran while one was open for 0% of the time, Pallas kernels for 0%

commit v1 on v0

--- a/solution.py
+++ b/solution.py
@@ -1,3 +1,4 @@
+import functools
 import math
 import jax
 import jax.numpy as jnp
@@ -6,6 +7,34 @@
 
 WINDOW_SAMPLES = 4096
 K = 32
+
+
+def supply_all_keys(z, k_dim):
+    newest = list(z.shape[1:])
+    newest[k_dim] *= z.shape[0]
+    return jnp.moveaxis(z, 0, k_dim).reshape(newest)
+
+
+def _recover_plate(body, axis_id):
+    axis_total = jax.lax.axis_size(axis_id)
+    met_up = body[None]
+    for k0 in range(axis_total.bit_length() - 1):
+        r2 = 1 << k0
+        blocks_here = []
+        for s in [*range(axis_total)]:
+            blocks_here.append((s, s ^ r2))
+        work_now = jax.lax.ppermute(met_up, axis_id, blocks_here)
+        s_next = jnp.stack([met_up, work_now])
+        wide_out = jax.lax.axis_index(axis_id) >> k0 & 1
+        met_up = jnp.where(wide_out == 0, s_next, s_next[::-1]).reshape(-1, *body.shape)
+    return met_up
+
+
+def end_sector_on(unit, xs, dim_at):
+    return supply_all_keys(_recover_plate(unit, xs), dim_at)
+
+
+scan_table = functools.partial(end_sector_on, xs="chan", dim_at=0)
 
 
 def dft_table(freqs, positions):
@@ -57,7 +86,7 @@
         tiled=True,
     )[0]
     panel = whiten(spectrum, chans, windows)
-    result = cross_block(panel, lax.all_gather(panel, "chan", axis=0, tiled=True))
+    result = cross_block(panel, scan_table(panel))
     return result[None]
 
 

time: 111 us -> 139 us (1.25)
  waiting for transfers between devices: 64.9 us -> 87.5 us
  starting transfers between devices: 0.04 us -> 5.68 us
    ppermute x0 -> x4, waiting for transfers between devices: none -> 64.3 us  [_recover_plate(): work_now = jax.lax.ppermute(met_up, axis_id, blocks_here)]
    all_gather x1 -> x0, waiting for transfers between devices: 41.6 us -> none  [shards(): lax.all_gather(panel, 'chan', axis=0, tiled=True)]
    ppermute x0 -> x4, starting transfers between devices: none -> 5.68 us  [_recover_plate(): work_now = jax.lax.ppermute(met_up, axis_id, blocks_here)]
    neg x1, other arithmetic: 1.89 us -> 0.25 us  [cross_block(): -other_panel[:, half_feat:]]
  transfers between devices with their start and end apart: 2 -> 5, of which waited for: 2 -> 5; matrix products, arithmetic and copies ran while one was open for 0% -> 0% of each run, Pallas kernels for 0% -> 0%
where the time goes in v1:
time: 139 us; the launch traced here: 138 us
  waiting for transfers between devices  87.5 us (63%)
  local copies, waits for them, and re-layouts  17.3 us (12%)
  between operations  13.5 us (10%)
  other arithmetic  7.71 us (6%)
  matrix products  6.48 us (5%)
  starting transfers between devices  5.68 us (4%)
    ppermute x4, waiting for transfers between devices, _recover_plate(): work_now = jax.lax.ppermute(met_up, axis_id, blocks_here)  64.3 us
    reduce_scatter x1, waiting for transfers between devices, shards(): lax.psum_scatter(partial_sum.reshape(chans * windows, own_rows * lax.axis...  23.3 us
    reshape x1, local copies, waits for them, and re-layouts, shards(): flat = strain.reshape(chans * windows, samp_dev)  6.86 us
    broadcast_in_dim x1, local copies, waits for them, and re-layouts, shards(): return result[None]  6.31 us
    ppermute x4, starting transfers between devices, _recover_plate(): work_now = jax.lax.ppermute(met_up, axis_id, blocks_here)  5.68 us
    dot_general x1, matrix products, shards(): jnp.dot(flat, table.reshape(samp_dev, own_rows * lax.axis_size('band') *...  3.73 us
  transfers between devices with their start and end apart: 5, of which 5 were waited for; matrix products, arithmetic and copies ran while one was open for 0% of the time, Pallas kernels for 0%

profile of v1, /device:TPU:0, one launch (start us, length us, event | category | flops | bytes accessed | tf_op | source)
XLA Modules:
  0.0 138.2 jit_solution(6035726031560936635)
XLA Ops:
  6.5 0.0 reduce-scatter.2.cloned.1.call-start
  6.5 0.1 multiply_subtract_fusion
  6.6 0.7 iota_add_fusion.1
  7.3 6.9 %reshape.82 = bf16[1024,2048]{1,0:T(8,128)(2,1)} reshape(bf16[256,4,2048]{2,1,0:T(4,128)(2,1)} %param.2) | data formatting | bytes 8388608 | tf_op jit(solution)/shard_map/reshape | solution.py:69
  14.2 2.3 %multiply_convert_fusion.3 = (bf16[2048,2,32]{0,2,1:T(8,128)(2,1)S(1)}, bf16[2048,2,32]{0,2,1:T(8,128)(2,1)S(1)}) fusion(s32[2,32]{1,0:T(2,128)S(1)} %iota_add_fusion.1, s32[2048]{0:T(1024)S(1)} %iota_add_fusion, f32[2048]{0:T(1024)S(1)} %get-tuple-element.11, f32[2048]{0:T(1024)S(1)} %get-tuple-element.12), kind=kLoop, calls=%fused_computation.26 | loop fusion | flops 2359296 | bytes 549120 | tf_op jit(solution)/shard_map/convert
  16.5 3.7 %fusion.12 = f32[128,1024]{1,0:T(8,128)S(1)} fusion(bf16[2048,128]{0,1:T(8,128)(2,1)S(1)} %bitcast.41, bf16[1024,2048]{1,0:T(8,128)(2,1)} %reshape.82), kind=kOutput, calls=%fused_computation.37 | convolution fusion | flops 536870912 | bytes 5242880 | tf_op jit(solution)/shard_map/dot_general | solution.py:75
  20.2 1.3 copy.5
  21.5 0.0 reduce-scatter.2.cloned.1.call-update
  21.6 23.3 %reduce-scatter.2.cloned.1.call-done = f32[1,1024,64]{2,1,0:T(8,128)} async-done(((f32[2,1024,64]{2,1,0:T(8,128)}), f32[1,1024,64]{2,1,0:T(8,128)}) %reduce-scatter.2.cloned.1.call-update) | async-done | bytes 262160 | tf_op jit(solution)/shard_map/reduce_scatter | solution.py:80
  44.8 1.2 multiply_reduce_fusion
  46.1 0.1 rsqrt.12
  46.2 1.7 %squeeze.3 = f32[256,4,2,32]{3,2,1,0:T(2,128)S(1)} reshape(f32[1,1024,64]{2,1,0:T(8,128)} %reduce-scatter.2.cloned.1.call-done) | data formatting | bytes 524288 | tf_op jit(solution)/shard_map/squeeze | solution.py:80
  47.9 1.7 %fusion.7 = bf16[256,2,4,32]{3,1,2,0:T(2,128)(2,1)S(1)} fusion(f32[256,4,2,32]{3,2,1,0:T(2,128)S(1)} %squeeze.3, f32[256,4]{1,0:T(8,128)S(1)} %rsqrt.12), kind=kLoop, calls=%fused_computation.21 | loop fusion | flops 131072 | bytes 397312 | tf_op jit(solution)/shard_map/transpose | solution.py:53
  49.6 0.5 copy.6
  50.1 0.1 collective-permute-start
  50.2 1.3 collective-permute-done
  51.5 0.1 fusion.9
  51.6 1.6 %collective-permute-start.1 = (bf16[2,256,256]{1,2,0:T(8,128)(2,1)S(1)}, bf16[2,256,256]{1,2,0:T(8,128)(2,1)S(1)}, u32[]{:S(2)}, u32[]{:S(2)}) collective-permute-start(bf16[2,256,256]{1,2,0:T(8,128)(2,1)S(1)} %get-tuple-element.8), channel_id=1, source_target_pairs={{0,4},{2,6},{4,0},{6,2},{8,12},{10,14},{12,8},{14,10},{16,20},{18,... | collective-permute-start | bytes 786440 | tf_op jit(solution)/shard_map/ppermute | solution.py:26
  53.2 6.9 %collective-permute-done.1 = bf16[2,256,256]{1,2,0:T(8,128)(2,1)S(1)} collective-permute-done((bf16[2,256,256]{1,2,0:T(8,128)(2,1)S(1)}, bf16[2,256,256]{1,2,0:T(8,128)(2,1)S(1)}, u32[]{:S(2)}, u32[]{:S(2)}) %collective-permute-start.1) | collective-permute-done | bytes 262176 | tf_op jit(solution)/shard_map/ppermute | solution.py:26
  60.0 0.1 pad_maximum_fusion.3
  60.1 0.1 reverse_select_fusion.2
  60.2 1.6 %collective-permute-start.2 = (bf16[4,256,256]{1,2,0:T(8,128)(2,1)S(1)}, bf16[4,256,256]{1,2,0:T(8,128)(2,1)S(1)}, u32[]{:S(2)}, u32[]{:S(2)}) collective-permute-start(bf16[4,256,256]{1,2,0:T(8,128)(2,1)S(1)} %bitcast.42), channel_id=1, source_target_pairs={{0,8},{2,10},{4,12},{6,14},{8,0},{10,2},{12,4},{14,6},{16,24},{18,... | collective-permute-start | bytes 1572872 | tf_op jit(solution)/shard_map/ppermute | solution.py:26
  61.8 11.6 %collective-permute-done.2 = bf16[4,256,256]{1,2,0:T(8,128)(2,1)S(1)} collective-permute-done((bf16[4,256,256]{1,2,0:T(8,128)(2,1)S(1)}, bf16[4,256,256]{1,2,0:T(8,128)(2,1)S(1)}, u32[]{:S(2)}, u32[]{:S(2)}) %collective-permute-start.2) | collective-permute-done | bytes 524320 | tf_op jit(solution)/shard_map/ppermute | solution.py:26
  73.4 0.1 pad_maximum_fusion.1
  73.5 0.2 reverse_select_fusion.1
  73.7 0.5 copy.8
  74.2 2.5 %collective-permute-start.3 = (bf16[8,256,256]{2,1,0:T(8,128)(2,1)S(1)}, bf16[8,256,256]{2,1,0:T(8,128)(2,1)S(1)}, u32[]{:S(2)}, u32[]{:S(2)}) collective-permute-start(bf16[8,256,256]{2,1,0:T(8,128)(2,1)S(1)} %bitcast.38), channel_id=1, source_target_pairs={{0,16},{2,18},{4,20},{6,22},{8,24},{10,26},{12,28},{14,30},{16,0},... | collective-permute-start | bytes 3145736 | tf_op jit(solution)/shard_map/ppermute | solution.py:26
  76.7 44.5 %collective-permute-done.3 = bf16[8,256,256]{2,1,0:T(8,128)(2,1)S(1)} collective-permute-done((bf16[8,256,256]{2,1,0:T(8,128)(2,1)S(1)}, bf16[8,256,256]{2,1,0:T(8,128)(2,1)S(1)}, u32[]{:S(2)}, u32[]{:S(2)}) %collective-permute-start.3) | collective-permute-done | bytes 1048608 | tf_op jit(solution)/shard_map/ppermute | solution.py:26
  121.1 0.2 pad_maximum_fusion
  121.3 0.5 reverse_select_fusion
  121.8 0.2 slice_negate_fusion
  122.1 0.2 maximum_bitcast_fusion
  122.3 2.7 %fusion = bf16[1,2,256,4096]{2,3,1,0:T(8,128)(2,1)} fusion(bf16[256,256,1]{0,1,2:T(8,128)(2,1)S(1)} %bitcast.47, bf16[1,4096,256]{2,1,0:T(8,128)(2,1)S(1)} %maximum_bitcast_fusion, bf16[1,4096,256]{2,1,0:T(8,128)(2,1)S(1)} %bitcast.36), kind=kOutput, calls=%fused_computation.1 | convolution fusion | flops 1080033280 | bytes 8519680 | tf_op jit(solution)/shard_map/gb,ozb->ogz/dot_general | solution.py:61
  125.0 6.3 %copy.12 = bf16[1,2,256,4096]{3,2,1,0:T(8,128)(2,1)} copy(bf16[1,2,256,4096]{2,3,1,0:T(8,128)(2,1)} %fusion) | data formatting | bytes 8388608 | tf_op jit(solution)/shard_map/broadcast_in_dim | solution.py:90
  (4 shorter events, 0.1 us)
Async XLA Ops:
  6.5 38.3 %reduce-scatter.2.cloned.1.call-start = ((), (), s32[]{:S(2)}) async-start(), calls=%async_computation.1 | async-start | bytes 1572864 | tf_op jit(solution)/shard_map/reduce_scatter | solution.py:80
  50.1 1.4 %collective-permute-start = (bf16[1,256,256]{1,2,0:T(8,128)(2,1)S(1)}, bf16[1,256,256]{1,2,0:T(8,128)(2,1)S(1)}, u32[]{:S(2)}, u32[]{:S(2)}) collective-permute-start(bf16[1,256,256]{1,2,0:T(8,128)(2,1)S(1)} %bitcast.45), channel_id=1, source_target_pairs={{0,2},{2,0},{4,6},{6,4},{8,10},{10,8},{12,14},{14,12},{16,18},{18,... | collective-permute-start | bytes 393224 | tf_op jit(solution)/shard_map/ppermute | solution.py:26
  51.6 8.4 %collective-permute-start.1 = (bf16[2,256,256]{1,2,0:T(8,128)(2,1)S(1)}, bf16[2,256,256]{1,2,0:T(8,128)(2,1)S(1)}, u32[]{:S(2)}, u32[]{:S(2)}) collective-permute-start(bf16[2,256,256]{1,2,0:T(8,128)(2,1)S(1)} %get-tuple-element.8), channel_id=1, source_target_pairs={{0,4},{2,6},{4,0},{6,2},{8,12},{10,14},{12,8},{14,10},{16,20},{18,... | collective-permute-start | bytes 786440 | tf_op jit(solution)/shard_map/ppermute | solution.py:26
  60.2 13.2 %collective-permute-start.2 = (bf16[4,256,256]{1,2,0:T(8,128)(2,1)S(1)}, bf16[4,256,256]{1,2,0:T(8,128)(2,1)S(1)}, u32[]{:S(2)}, u32[]{:S(2)}) collective-permute-start(bf16[4,256,256]{1,2,0:T(8,128)(2,1)S(1)} %bitcast.42), channel_id=1, source_target_pairs={{0,8},{2,10},{4,12},{6,14},{8,0},{10,2},{12,4},{14,6},{16,24},{18,... | collective-permute-start | bytes 1572872 | tf_op jit(solution)/shard_map/ppermute | solution.py:26
  74.2 46.9 %collective-permute-start.3 = (bf16[8,256,256]{2,1,0:T(8,128)(2,1)S(1)}, bf16[8,256,256]{2,1,0:T(8,128)(2,1)S(1)}, u32[]{:S(2)}, u32[]{:S(2)}) collective-permute-start(bf16[8,256,256]{2,1,0:T(8,128)(2,1)S(1)} %bitcast.38), channel_id=1, source_target_pairs={{0,16},{2,18},{4,20},{6,22},{8,24},{10,26},{12,28},{14,30},{16,0},... | collective-permute-start | bytes 3145736 | tf_op jit(solution)/shard_map/ppermute | solution.py:26
Sparse Core Ops, SparseCore 0:
  21.7 23.0 reduce-scatter.1
